TPU v7x, 32 devices: a whole 2x2x4 slice. The times are simulated.
32 devices in a mesh: clus: 4 (over y, x), fsdp: 4 (over z), head: 2 (over core).
Axes of the slice: x: 2, y: 2, z: 4, core: 2. Of those that a mesh axis runs over, the one named last changes fastest.
Arguments:
- feats: bfloat16 [4096, 2048], P(('clus', 'fsdp')), as said below
- w_query: float32 [2048, 2048], P(('clus', 'fsdp'), 'head'), may hold values from -0.125 to 0.125
- w_keyval: float32 [2048, 2048], P(('clus', 'fsdp'), 'head'), may hold values from -0.125 to 0.125
- grad_out: bfloat16 [4096, 2048], P(('clus', 'fsdp'), 'head'), may hold values from -6 to 6
- col_block: int32 [32, 5], replicated, may hold values from 0 to 31, as said below
- col_count: int32 [32], replicated, may hold values from 4 to 5
Outputs:
- out: bfloat16 [4096, 2048], P(('clus', 'fsdp'), 'head')
- grad_w_query: float32 [2048, 2048], P(('clus', 'fsdp'), 'head')
- grad_w_keyval: float32 [2048, 2048], P(('clus', 'fsdp'), 'head')
Inputs may be any that keep to these rules, and one draw needn't show every extreme that they name: `col_block`: column 0 of row b is b itself; column 1 is another block of b's cluster (cluster of a block = block // 2); the other columns lie in other clusters whose index differs from b's cluster by a nonzero multiple of 4. A row names each block at most once. The rows of one cluster name, in any other cluster, at most one distinct block. `feats`: node features of order one, rows of differing scale.
All inputs are finite; a program needn't handle non-finite values.
Results may differ from a plain program's by a relative error of at most 0.014.
The roundings to bfloat16 on the way count: a program that leaves them out, or rounds other values in their place, can miss the bound.
Values may be sent and summed in bfloat16 or wider, within the bound.
No kernel may reach another device: no remote copies, remote signals or barrier semaphores. Data moves between devices by JAX's collectives and lax.ppermute only.
A program may use at most 128 MiB of HBM per device.

v0:
```python
import math

import jax
import jax.numpy as jnp
from jax import lax
from jax.sharding import PartitionSpec as P

HD = 128
BLK = 128
NCOL = 5


def on_device(feats, w_query, w_keyval, grad_out, col_block, col_count):
    rows = feats.shape[0]
    half = w_query.shape[1]
    nlocal = rows // BLK
    heads_here = half // HD
    nclus = lax.axis_size("clus")
    nfsdp = lax.axis_size("fsdp")
    clus_at = lax.axis_index("clus")
    fsdp_at = lax.axis_index("fsdp")
    myself = clus_at * nfsdp + fsdp_at
    scale = 1.0 / math.sqrt(HD)
    columns = feats
    acc_query = jnp.dot(
        columns,
        lax.all_gather(w_query.astype(jnp.bfloat16), ("clus", "fsdp"), axis=0, tiled=True),
        preferred_element_type=jnp.float32,
    )
    acc_keyval = jnp.dot(
        columns,
        lax.all_gather(w_keyval.astype(jnp.bfloat16), ("clus", "fsdp"), axis=0, tiled=True),
        preferred_element_type=jnp.float32,
    )
    query = acc_query.astype(jnp.bfloat16)
    keyval = acc_keyval.astype(jnp.bfloat16)
    all_cols = col_block.reshape(nclus, nfsdp, nlocal, NCOL)
    all_counts = col_count.reshape(nclus, nfsdp, nlocal)
    peer_cols = lax.dynamic_index_in_dim(all_cols, fsdp_at, 1, keepdims=False)
    peer_counts = lax.dynamic_index_in_dim(all_counts, fsdp_at, 1, keepdims=False)
    peer_live = jnp.arange(NCOL, dtype=jnp.int32)[None, None, :] < peer_counts[:, :, None]
    my_blocks = myself * nlocal + jnp.arange(nlocal, dtype=jnp.int32)
    listed = (peer_cols[:, :, :, None] == my_blocks[None, None, None, :]) & peer_live[:, :, :, None]
    needed = jnp.any(listed, axis=(1, 2)) & (jnp.arange(nclus, dtype=jnp.int32) != clus_at)[:, None]
    flat_keyval = keyval.reshape(nlocal, BLK * half)
    outgoing = jnp.dot(needed.astype(jnp.bfloat16), flat_keyval, preferred_element_type=jnp.float32)
    outgoing = outgoing.astype(jnp.bfloat16).reshape(nclus, BLK, half)
    received = lax.all_to_all(outgoing, "clus", split_axis=0, concat_axis=0, tiled=True)
    my_cols = lax.dynamic_slice_in_dim(col_block, myself * nlocal, nlocal, 0)
    my_counts = lax.dynamic_slice_in_dim(col_count, myself * nlocal, nlocal, 0)
    col_cluster = my_cols // nlocal
    inside = col_cluster == myself
    table_index = jnp.where(inside, my_cols % nlocal, nlocal + col_cluster // nfsdp).reshape(-1)
    table = jnp.concatenate([keyval.reshape(nlocal, BLK, half), received], 0)
    keys = jnp.take(table, table_index, axis=0).reshape(nlocal, NCOL * BLK, heads_here, HD)
    queries = query.reshape(nlocal, BLK, heads_here, HD)
    cotans = grad_out.reshape(nlocal, BLK, heads_here, HD)
    valid = jnp.repeat(jnp.arange(NCOL, dtype=jnp.int32)[None, :] < my_counts[:, None], BLK, axis=1)
    score = jnp.einsum("bqhd,bkhd->bhqk", queries, keys, preferred_element_type=jnp.float32) * scale
    score = jnp.where(valid[:, None, None, :], score, -1e30)
    top = jnp.max(score, axis=-1, keepdims=True)
    expo = jnp.exp(score - top)
    prob = expo / jnp.sum(expo, axis=-1, keepdims=True)
    prob_b = prob.astype(jnp.bfloat16)
    out = (
        jnp.einsum("bhqk,bkhd->bqhd", prob_b, keys, preferred_element_type=jnp.float32)
        .astype(jnp.bfloat16)
        .reshape(rows, half)
    )
    dprob = jnp.einsum("bqhd,bkhd->bhqk", cotans, keys, preferred_element_type=jnp.float32)
    delta = jnp.sum(prob * dprob, axis=-1, keepdims=True)
    dscore = (prob * (dprob - delta)).astype(jnp.bfloat16)
    dquery = (
        (jnp.einsum("bhqk,bkhd->bqhd", dscore, keys, preferred_element_type=jnp.float32) * scale)
        .astype(jnp.bfloat16)
        .reshape(rows, half)
    )
    dkeys = (
        jnp.einsum("bhqk,bqhd->bkhd", dscore, queries, preferred_element_type=jnp.float32) * scale
    )
    dkeys = dkeys + jnp.einsum(
        "bhqk,bqhd->bkhd", prob_b, cotans, preferred_element_type=jnp.float32
    )
    dkeys = dkeys.reshape(nlocal * NCOL, BLK * half)
    onehot = (table_index[:, None] == jnp.arange(nlocal + nclus, dtype=jnp.int32)[None, :]).astype(
        jnp.float32
    )
    grad_table = jnp.dot(onehot.T, dkeys, precision=lax.Precision.HIGHEST)
    returned = lax.all_to_all(
        grad_table[nlocal:].reshape(nclus, BLK, half),
        "clus",
        split_axis=0,
        concat_axis=0,
        tiled=True,
    )
    dkeyval = grad_table[:nlocal] + jnp.dot(
        needed.T.astype(jnp.float32),
        returned.reshape(nclus, BLK * half),
        precision=lax.Precision.HIGHEST,
    )
    dkeyval = dkeyval.astype(jnp.bfloat16).reshape(rows, half)
    both_grads = jnp.concatenate([dquery, dkeyval], 1)
    columns = feats
    partial_sum = lax.psum_scatter(
        lax.dot_general(
            columns, both_grads, (((0,), (0,)), ((), ())), preferred_element_type=jnp.float32
        ).astype(jnp.bfloat16),
        "clus",
        scatter_dimension=0,
        tiled=True,
    ).astype(jnp.float32)
    final = lax.psum_scatter(partial_sum, "fsdp", scatter_dimension=0, tiled=True)
    return (out, final[:, :half], final[:, half:])


def solution(mesh):
    return jax.shard_map(
        on_device,
        mesh=mesh,
        in_specs=(
            P(("clus", "fsdp"), None),
            P(("clus", "fsdp"), "head"),
            P(("clus", "fsdp"), "head"),
            P(("clus", "fsdp"), "head"),
            P(),
            P(),
        ),
        out_specs=(
            P(("clus", "fsdp"), "head"),
            P(("clus", "fsdp"), "head"),
            P(("clus", "fsdp"), "head"),
        ),
        check_vma=False,
    )
```

profile of v0, /device:TPU:0, one launch (start us, length us, event | category | flops | bytes accessed | tf_op | source)
XLA Modules:
  0.0 432.5 jit_solution(14793462806135537929)
XLA Ops:
  14.7 75.0 %all-gather.3.cloned.1.call-done = bf16[2048,1024]{1,0:T(8,128)(2,1)} async-done(((bf16[128,1024]{1,0:T(8,128)(2,1)}), bf16[2048,1024]{1,0:T(8,128)(2,1)}) %all-gather.3.cloned.1.call-update) | async-done | bytes 4194320 | tf_op jit(solution)/shard_map/all_gather | solution.py:32
  89.7 3.4 convolution_convert_fusion.2
  95.9 3.7 all-to-all-start
  100.8 70.4 %all-gather.5.cloned.1.call-done = bf16[2048,1024]{1,0:T(8,128)(2,1)} async-done(((bf16[128,1024]{1,0:T(8,128)(2,1)}), bf16[2048,1024]{1,0:T(8,128)(2,1)}) %all-gather.5.cloned.1.call-update) | async-done | bytes 4194320 | tf_op jit(solution)/shard_map/all_gather | solution.py:27
  171.2 3.4 fusion.21
  177.6 2.4 gather_fusion
  180.0 2.4 copy.75
  182.4 2.7 bitcast_select_fusion
  193.4 3.0 bitcast_add_fusion
  196.4 6.2 %copy.67 = f32[2,640,8,128]{3,2,1,0:T(8,128)} copy(f32[2,640,8,128]{1,3,2,0:T(8,128)} %bitcast_add_fusion) | data formatting | bytes 10485760 | tf_op jit(solution)/shard_map/add | solution.py:81
  202.7 6.2 %reshape.121 = f32[10,131072]{1,0:T(8,128)} reshape(f32[2,640,8,128]{3,2,1,0:T(8,128)} %copy.67) | data formatting | bytes 10485760 | tf_op jit(solution)/shard_map/reshape | solution.py:84
  208.8 5.7 %fusion.30 = f32[6,131072]{1,0:T(8,128)S(1)} fusion(f32[10,131072]{1,0:T(8,128)} %reshape.121, s32[10]{0:T(128)S(1)} %reshape.120), kind=kOutput, calls=%fused_computation.49 | convolution fusion | flops 94371904 | bytes 8388648 | tf_op jit(solution)/shard_map/dot_general | solution.py:88
  215.1 2.6 copy.101
  217.7 3.6 all-to-all-start.1
  221.3 4.8 %copy.55 = bf16[2,640,8,128]{1,3,2,0:T(8,128)(2,1)} copy(bf16[2,640,8,128]{3,2,1,0:T(8,128)(2,1)} %copy-done.3) | data formatting | bytes 5242880 | tf_op jit(solution)/shard_map/jit(_take)/select_n | solution.py:55
  226.2 4.4 %fusion.20 = bf16[2,128,8,128]{1,3,2,0:T(8,128)(2,1)} fusion(bf16[2,640,8,128]{1,3,2,0:T(8,128)(2,1)} %copy.55, bf16[2,8,128,640]{3,2,1,0:T(8,128)(2,1)} %copy-done.4), kind=kOutput, calls=%fused_computation.34 | convolution fusion | flops 336068608 | bytes 5767168 | tf_op jit(solution)/shard_map/bhqk,bkhd->bqhd/dot_general | solution.py:74
  230.6 2.1 copy.61
  234.6 10.2 %all-to-all-done.1 = f32[4,128,1024]{2,1,0:T(8,128)S(1)} async-done(((f32[4,128,1024]{2,1,0:T(8,128)}), f32[4,128,1024]{2,1,0:T(8,128)S(1)}, u32[]{:S(2)}, u32[]{:S(2)}) %all-to-all-start.1) | async-done | bytes 2097184 | tf_op jit(solution)/shard_map/all_to_all | solution.py:89
  246.9 2.6 fusion.1
  250.0 5.6 %convert_bitcast_fusion = bf16[2048,2048]{0,1:T(8,128)(2,1)} fusion(bf16[256,2048]{1,0:T(8,128)(2,1)S(1)} %copy-done, bf16[256,1024]{1,0:T(8,128)(2,1)S(1)} %reshape.124, bf16[256,1024]{1,0:T(8,128)(2,1)S(1)} %bitcast.95), kind=kOutput, calls=%fused_computation.5 | convolution fusion | flops 2153775104 | bytes 10485760 | tf_op jit(solution)/shard_map/dot_general | solution.py:105
  255.7 85.9 %reduce-scatter.3.cloned.1.call-done = bf16[512,2048]{0,1:T(8,128)(2,1)} async-done(((bf16[2048,2048]{0,1:T(8,128)(2,1)}), bf16[512,2048]{0,1:T(8,128)(2,1)}) %reduce-scatter.3.cloned.1.call-update) | async-done | bytes 2097168 | tf_op jit(solution)/shard_map/reduce_scatter | solution.py:104
  341.6 4.1 convert_element_type.62
  345.8 4.4 %fusion.22 = bf16[2,128,8,128]{1,3,2,0:T(8,128)(2,1)S(1)} fusion(bf16[2,640,8,128]{1,3,2,0:T(8,128)(2,1)} %copy.55, f32[2,8,128,640]{3,2,1,0:T(8,128)} %copy-done.5, f32[2,8,128]{2,1,0:T(8,128)S(1)} %get-tuple-element.16), kind=kOutput, calls=%fused_computation.36 | convolution fusion | flops 338427904 | bytes 8396800 | tf_op jit(solution)/shard_map/bhqk,bkhd->bqhd/dot_general | solution.py:66
  351.4 71.3 %reduce-scatter.5.cloned.1.call-done = f32[128,2048]{0,1:T(8,128)} async-done(((f32[512,2048]{0,1:T(8,128)}), f32[128,2048]{0,1:T(8,128)}) %reduce-scatter.5.cloned.1.call-update) | async-done | bytes 1048592 | tf_op jit(solution)/shard_map/reduce_scatter | solution.py:112
  (77 shorter events, 32.4 us)
Async XLA Ops:
  7.2 82.5 %copy-start = (bf16[256,2048]{1,0:T(8,128)(2,1)S(1)}, bf16[256,2048]{1,0:T(8,128)(2,1)}, u32[]{:S(2)}) copy-start(bf16[256,2048]{1,0:T(8,128)(2,1)} %param.6) | copy-start | bytes 3145732
  7.2 82.5 %all-gather.3.cloned.1.call-start = ((), (), s32[]{:S(2)}) async-start(), calls=%async_computation.4 | async-start | bytes 4456448 | tf_op jit(solution)/shard_map/all_gather | solution.py:32
  9.1 162.1 %all-gather.5.cloned.1.call-start = ((), (), s32[]{:S(2)}) async-start(), calls=%async_computation.5 | async-start | bytes 4456448 | tf_op jit(solution)/shard_map/all_gather | solution.py:27
  93.1 2.8 copy-start.7
  93.5 6.4 %copy-start.9 = (bf16[256,1024]{1,0:T(8,128)(2,1)S(1)}, bf16[256,1024]{1,0:T(8,128)(2,1)}, u32[]{:S(2)}) copy-start(bf16[256,1024]{1,0:T(8,128)(2,1)} %param.9) | copy-start | bytes 1572868
  95.9 79.3 %all-to-all-start = ((bf16[4,128,1024]{2,1,0:T(8,128)(2,1)}), bf16[4,128,1024]{2,1,0:T(8,128)(2,1)S(1)}, u32[]{:S(2)}, u32[]{:S(2)}) async-start(bf16[4,128,1024]{2,1,0:T(8,128)(2,1)} %bitcast.79), calls=%async_computation | async-start | bytes 2097152 | tf_op jit(solution)/shard_map/all_to_all | solution.py:48
  175.2 1.0 copy-start.6
  185.1 3.0 copy-start.3
  186.1 1.9 copy-start.10
  188.0 5.4 %copy-start.5 = (f32[2,8,128,640]{3,2,1,0:T(8,128)}, f32[2,8,128,640]{3,2,1,0:T(8,128)S(1)}, u32[]{:S(2)}) copy-start(f32[2,8,128,640]{3,2,1,0:T(8,128)S(1)} %get-tuple-element.17) | copy-start | bytes 15728644
  191.1 1.5 copy-start.4
  214.5 3.1 copy-start.1
  217.7 27.1 %all-to-all-start.1 = ((f32[4,128,1024]{2,1,0:T(8,128)}), f32[4,128,1024]{2,1,0:T(8,128)S(1)}, u32[]{:S(2)}, u32[]{:S(2)}) async-start(f32[4,128,1024]{2,1,0:T(8,128)} %bitcast.88), calls=%async_computation.1 | async-start | bytes 4194304 | tf_op jit(solution)/shard_map/all_to_all | solution.py:89
  221.3 120.3 %reduce-scatter.3.cloned.1.call-start = ((), (), s32[]{:S(2)}) async-start(), calls=%async_computation.6 | async-start | bytes 10485760 | tf_op jit(solution)/shard_map/reduce_scatter | solution.py:104
  244.8 2.2 copy-start.2
  246.1 3.9 copy-start.8
  255.6 167.1 %reduce-scatter.5.cloned.1.call-start = ((), (), s32[]{:S(2)}) async-start(), calls=%async_computation.7 | async-start | bytes 5242880 | tf_op jit(solution)/shard_map/reduce_scatter | solution.py:112
Sparse Core Ops, SparseCore 0:
  11.3 78.2 all-gather.2
  93.0 78.2 all-gather.4
  255.8 85.8 reduce-scatter.2
  345.9 76.7 reduce-scatter.4
where the time goes:
time: 433 us
  waiting for transfers between devices  313 us (72%)
  local copies, waits for them, and re-layouts  44.6 us (10%)
  matrix products  37.6 us (9%)
  other arithmetic  15.9 us (4%)
  between operations  14.1 us (3%)
  starting transfers between devices  7.47 us (2%)
    reduce_scatter x1, waiting for transfers between devices, on_device(): lax.psum_scatter(lax.dot_general(columns, both_grads, (((0,), (0,)), ((),...  85.9 us
    all_gather x1, waiting for transfers between devices, on_device(): lax.all_gather(w_keyval.astype(jnp.bfloat16), ('clus', 'fsdp'), axis=0, t...  75 us
    reduce_scatter x1, waiting for transfers between devices, on_device(): lax.psum_scatter(partial_sum, 'fsdp', scatter_dimension=0, tiled=True)  71.3 us
    all_gather x1, waiting for transfers between devices, on_device(): lax.all_gather(w_query.astype(jnp.bfloat16), ('clus', 'fsdp'), axis=0, ti...  70.4 us
    unnamed x37, local copies, waits for them, and re-layouts  17.6 us
    all_to_all x1, waiting for transfers between devices, on_device(): lax.all_to_all(grad_table[nlocal:].reshape(nclus, BLK, half), 'clus', spl...  10.2 us
  transfers between devices with their start and end apart: 6, of which 5 were waited for; matrix products, arithmetic and copies ran while one was open for 8% of the time, Pallas kernels for 0%

commit v1 on v0

--- a/solution.py
+++ b/solution.py
@@ -3,11 +3,292 @@
 import jax
 import jax.numpy as jnp
 from jax import lax
+from jax.experimental import pallas as pl
+from jax.experimental.pallas import tpu as pltpu
 from jax.sharding import PartitionSpec as P
 
 HD = 128
 BLK = 128
 NCOL = 5
+
+ANY = pl.BlockSpec(memory_space=pl.ANY)
+SMEM = pl.BlockSpec(memory_space=pltpu.SMEM)
+VMEM = pl.BlockSpec(memory_space=pltpu.VMEM)
+
+
+def split_weights(wq_ref, wkv_ref, *out_refs):
+    slots = len(out_refs)
+    for j, out_ref in enumerate(out_refs):
+        for d in range(out_ref.shape[0]):
+            at = (d * slots + j) * HD
+            out_ref[d, :, :HD] = wq_ref[:, at : at + HD].astype(jnp.bfloat16)
+            out_ref[d, :, HD:] = wkv_ref[:, at : at + HD].astype(jnp.bfloat16)
+
+
+def split_heads(x_ref, *out_refs):
+    slots = len(out_refs)
+    for j, out_ref in enumerate(out_refs):
+        for d in range(out_ref.shape[0]):
+            at = (d * slots + j) * HD
+            out_ref[d] = x_ref[:, at : at + HD]
+
+
+def merge_heads(*refs):
+    *in_refs, out_ref = refs
+    slots = len(in_refs)
+    for j, in_ref in enumerate(in_refs):
+        for d in range(in_ref.shape[0]):
+            at = (d * slots + j) * HD
+            out_ref[:, at : at + HD] = in_ref[d]
+
+
+def merge_grads(*refs):
+    *in_refs, gq_ref, gkv_ref = refs
+    slots = len(in_refs)
+    for j, in_ref in enumerate(in_refs):
+        for d in range(in_ref.shape[0]):
+            at = (d * slots + j) * HD
+            gq_ref[:, at : at + HD] = in_ref[d, :HD, :].astype(jnp.float32).T
+            gkv_ref[:, at : at + HD] = in_ref[d, HD:, :].astype(jnp.float32).T
+
+
+def head_kernel(
+    pos_ref,
+    cols_ref,
+    counts_ref,
+    feats_ref,
+    mine1_ref,
+    mine2_ref,
+    mine3_ref,
+    other1_ref,
+    other2_ref,
+    other3_ref,
+    w0_ref,
+    wup_ref,
+    wdn_ref,
+    wfar_up_ref,
+    wfar_dn_ref,
+    cotan_ref,
+    out_ref,
+    grad0_ref,
+    grad1_ref,
+    grad2_ref,
+    grad3_ref,
+    f_ref,
+    w_ref,
+    g_ref,
+    qkv_ref,
+    dkv_ref,
+    dqkv_ref,
+    grad_ref,
+    sems,
+    out_sems,
+):
+    clus_at = pos_ref[0]
+    fsdp_at = pos_ref[1]
+    head_at = pos_ref[2]
+    rows, width = feats_ref.shape
+    half = width // 2
+    nodes = f_ref.shape[0]
+    scale = 1.0 / math.sqrt(HD)
+    feat_copies = [
+        pltpu.make_async_copy(feats_ref, f_ref.at[pl.ds(pl.multiple_of(clus_at * rows, rows), rows), :], sems.at[0])
+    ]
+    for m, (mine, other) in enumerate(
+        ((mine1_ref, other1_ref), (mine2_ref, other2_ref), (mine3_ref, other3_ref)), 1
+    ):
+        at = pl.ds(pl.multiple_of((clus_at ^ m) * rows, rows), rows)
+        feat_copies.append(
+            pltpu.make_async_copy(
+                mine, f_ref.at[at, pl.ds(pl.multiple_of(head_at * half, half), half)], sems.at[m]
+            )
+        )
+        feat_copies.append(
+            pltpu.make_async_copy(
+                other, f_ref.at[at, pl.ds(pl.multiple_of((1 - head_at) * half, half), half)], sems.at[m + 3]
+            )
+        )
+    near = [
+        pltpu.make_async_copy(w0_ref, w_ref.at[:, fsdp_at], sems.at[7]),
+        pltpu.make_async_copy(wup_ref, w_ref.at[:, (fsdp_at + 3) % 4], sems.at[8]),
+        pltpu.make_async_copy(wdn_ref, w_ref.at[:, (fsdp_at + 1) % 4], sems.at[9]),
+        pltpu.make_async_copy(cotan_ref, g_ref, sems.at[11]),
+    ]
+    far_up = pltpu.make_async_copy(wfar_up_ref, w_ref.at[:, (fsdp_at + 2) % 4], sems.at[10])
+    far_dn = pltpu.make_async_copy(wfar_dn_ref, w_ref.at[:, (fsdp_at + 2) % 4], sems.at[10])
+    for copy in feat_copies + near:
+        copy.start()
+
+    @pl.when(fsdp_at >= 2)
+    def _():
+        far_up.start()
+        far_up.wait()
+
+    @pl.when(fsdp_at < 2)
+    def _():
+        far_dn.start()
+        far_dn.wait()
+
+    dkv_ref[...] = jnp.zeros_like(dkv_ref)
+    for copy in feat_copies + near:
+        copy.wait()
+    weights = w_ref[...].reshape(width, 2 * HD)
+    for r in range(nodes // rows):
+        at = slice(r * rows, (r + 1) * rows)
+        qkv_ref[at, :] = jnp.dot(f_ref[at, :], weights, preferred_element_type=jnp.float32).astype(
+            jnp.bfloat16
+        )
+    nt = (((1,), (1,)), ((), ()))
+    tn = (((0,), (0,)), ((), ()))
+    place = lax.broadcasted_iota(jnp.int32, (BLK, NCOL * BLK), 1)
+    for b in range(nodes // BLK):
+        at = slice(b * BLK, (b + 1) * BLK)
+        query = qkv_ref[at, :HD]
+        cotan = g_ref[at, :]
+        listed = [pl.ds(pl.multiple_of(cols_ref[b, n] * BLK, BLK), BLK) for n in range(NCOL)]
+        keys = jnp.concatenate([qkv_ref[rows_at, HD:] for rows_at in listed], 0)
+        score = lax.dot_general(query, keys, nt, preferred_element_type=jnp.float32) * scale
+        score = jnp.where(place < counts_ref[b] * BLK, score, -1e30)
+        top = jnp.max(score, axis=-1, keepdims=True)
+        expo = jnp.exp(score - top)
+        prob = expo / jnp.sum(expo, axis=-1, keepdims=True)
+        prob_b = prob.astype(jnp.bfloat16)
+        out_ref[at, :] = jnp.dot(prob_b, keys, preferred_element_type=jnp.float32).astype(jnp.bfloat16)
+        dprob = lax.dot_general(cotan, keys, nt, preferred_element_type=jnp.float32)
+        delta = jnp.sum(prob * dprob, axis=-1, keepdims=True)
+        dscore = (prob * (dprob - delta)).astype(jnp.bfloat16)
+        dqkv_ref[at, :HD] = (
+            jnp.dot(dscore, keys, preferred_element_type=jnp.float32) * scale
+        ).astype(jnp.bfloat16)
+        dkeys = lax.dot_general(dscore, query, tn, preferred_element_type=jnp.float32) * scale
+        dkeys = dkeys + lax.dot_general(prob_b, cotan, tn, preferred_element_type=jnp.float32)
+        for n, rows_at in enumerate(listed):
+            dkv_ref[rows_at, :] = dkv_ref[rows_at, :] + dkeys[n * BLK : (n + 1) * BLK]
+    dqkv_ref[:, HD:] = dkv_ref[...].astype(jnp.bfloat16)
+    planes, owners = grad_ref.shape[:2]
+    step = width // owners
+    part = step // planes
+    for s in range(owners):
+        term = lax.dot_general(
+            dqkv_ref[...], f_ref[:, s * step : (s + 1) * step], tn, preferred_element_type=jnp.float32
+        ).astype(jnp.bfloat16)
+        for f in range(planes):
+            grad_ref[f, s] = term[:, f * part : (f + 1) * part]
+    copies = [
+        pltpu.make_async_copy(grad_ref.at[(fsdp_at + k) % 4], ref, out_sems.at[k])
+        for k, ref in enumerate((grad0_ref, grad1_ref, grad2_ref, grad3_ref))
+    ]
+    for copy in copies:
+        copy.start()
+    for copy in copies:
+        copy.wait()
+
+
+def in_plane(feats, w_query, w_keyval, grad_out, col_block, col_count):
+    rows, width = feats.shape
+    wrows, half = w_query.shape
+    nlocal = rows // BLK
+    nclus = lax.axis_size("clus")
+    nfsdp = lax.axis_size("fsdp")
+    slots = half // HD // nclus
+    clus_at = lax.axis_index("clus")
+    fsdp_at = lax.axis_index("fsdp")
+    head_at = lax.axis_index("head")
+    nodes = nclus * rows
+    bf16 = jnp.bfloat16
+
+    def shape(dims, dtype=bf16):
+        return jax.ShapeDtypeStruct(dims, dtype)
+
+    def shift(x, pairs):
+        return lax.ppermute(x, "fsdp", pairs)
+
+    up_ring = [(i, (i + 1) % nfsdp) for i in range(nfsdp)]
+    dn_ring = [(i, (i - 1) % nfsdp) for i in range(nfsdp)]
+    parts = pl.pallas_call(
+        split_weights,
+        in_specs=[VMEM] * 2,
+        out_specs=[VMEM] * slots,
+        out_shape=[shape((nclus, wrows, 2 * HD))] * slots,
+        name="split_weights",
+    )(w_query, w_keyval)
+    own_w = [lax.all_to_all(x, "clus", 0, 0, tiled=True) for x in parts]
+    mine = lax.dynamic_slice_in_dim(feats, head_at * (width // 2), width // 2, 1)
+    near = [lax.ppermute(mine, "clus", [(i, i ^ m) for i in range(nclus)]) for m in (1, 2, 3)]
+    far = [lax.ppermute(x, "head", [(0, 1), (1, 0)]) for x in near]
+    cotans = pl.pallas_call(
+        split_heads,
+        in_specs=[VMEM],
+        out_specs=[VMEM] * slots,
+        out_shape=[shape((nclus, rows, HD))] * slots,
+        name="split_cotans",
+    )(grad_out)
+    cotans = [lax.all_to_all(x, "clus", 0, 0, tiled=True).reshape(nodes, HD) for x in cotans]
+    all_cols = col_block.reshape(nclus, nfsdp, nlocal, NCOL)
+    cols = lax.dynamic_index_in_dim(all_cols, fsdp_at, 1, keepdims=False).reshape(nclus * nlocal, NCOL)
+    cols = cols // nlocal // nfsdp * nlocal + cols % nlocal
+    counts = lax.dynamic_index_in_dim(
+        col_count.reshape(nclus, nfsdp, nlocal), fsdp_at, 1, keepdims=False
+    ).reshape(nclus * nlocal)
+    pos = jnp.stack([clus_at, fsdp_at, head_at]).astype(jnp.int32)
+    outs = []
+    grads = []
+    piece = (nclus, 2 * HD, wrows)
+    for j in range(slots):
+        w0 = own_w[j]
+        wup = shift(w0, up_ring)
+        wdn = shift(w0, dn_ring)
+        wfar_up = shift(wup, [(1, 2), (2, 3)])
+        wfar_dn = shift(wdn, [(2, 1), (1, 0)])
+        out, g0, g1, g2, g3 = pl.pallas_call(
+            head_kernel,
+            in_specs=[SMEM] * 3 + [ANY] * 13,
+            out_specs=[VMEM] + [ANY] * 4,
+            out_shape=[shape((nodes, HD))] + [shape(piece)] * 4,
+            scratch_shapes=[
+                pltpu.VMEM((nodes, width), bf16),
+                pltpu.VMEM((nclus, nfsdp, wrows, 2 * HD), bf16),
+                pltpu.VMEM((nodes, HD), bf16),
+                pltpu.VMEM((nodes, 2 * HD), bf16),
+                pltpu.VMEM((nodes, HD), jnp.float32),
+                pltpu.VMEM((nodes, 2 * HD), bf16),
+                pltpu.VMEM((nfsdp,) + piece, bf16),
+                pltpu.SemaphoreType.DMA((12,)),
+                pltpu.SemaphoreType.DMA((4,)),
+            ],
+            name="heads",
+        )(pos, cols, counts, feats, *near, *far, w0, wup, wdn, wfar_up, wfar_dn, cotans[j])
+        outs.append(lax.all_to_all(out.reshape(nclus, rows, HD), "clus", 0, 0, tiled=True))
+        far_a = shift(g3, [(0, 3)])
+        far_b = shift(g1, [(3, 0)])
+        up1 = shift(g2, [(0, 1), (1, 2)])
+        dn1 = shift(g2, [(3, 2), (2, 1)])
+        up2 = shift(add(g1, up1), [(0, 1), (1, 2), (2, 3)])
+        dn2 = shift(add(g3, dn1), [(3, 2), (2, 1), (1, 0)])
+        total = add(g0, up2, dn2, far_a, far_b)
+        grads.append(lax.all_to_all(total, "clus", 0, 0, tiled=True))
+    out = pl.pallas_call(
+        merge_heads,
+        in_specs=[VMEM] * slots,
+        out_specs=VMEM,
+        out_shape=shape((rows, half)),
+        name="merge_out",
+    )(*outs)
+    gq, gkv = pl.pallas_call(
+        merge_grads,
+        in_specs=[VMEM] * slots,
+        out_specs=[VMEM] * 2,
+        out_shape=[shape((wrows, half), jnp.float32)] * 2,
+        name="merge_grads",
+    )(*grads)
+    return out, gq, gkv
+
+
+def add(*xs):
+    total = xs[0].astype(jnp.float32)
+    for x in xs[1:]:
+        total = total + x.astype(jnp.float32)
+    return total.astype(jnp.bfloat16)
 
 
 def on_device(feats, w_query, w_keyval, grad_out, col_block, col_count):
@@ -114,8 +395,9 @@
 
 
 def solution(mesh):
+    square = mesh.shape["clus"] == 4 and mesh.shape["fsdp"] == 4 and mesh.shape["head"] == 2
     return jax.shard_map(
-        on_device,
+        in_plane if square else on_device,
         mesh=mesh,
         in_specs=(
             P(("clus", "fsdp"), None),

time: 433 us -> 175 us (0.40)
  waiting for transfers between devices: 313 us -> 24.1 us
  starting transfers between devices: 7.47 us -> 77.2 us
  local copies, waits for them, and re-layouts: 44.6 us -> 6.4 us
  matrix products: 37.6 us -> 0 us
  Pallas kernels: 0 us -> 37.3 us
  blocking collectives: 0 us -> 20.7 us
  between operations: 14.1 us -> 1.11 us
  other arithmetic: 15.9 us -> 5.34 us
    reduce_scatter x2 -> x0, waiting for transfers between devices: 157 us -> none  [the longest x1 85.9 us: on_device(): lax.psum_scatter(lax.dot_general(columns, both_grads, (((0,), (0,)), ((),...]
    all_gather x2 -> x0, waiting for transfers between devices: 145 us -> none  [the longest x1 75 us: on_device(): lax.all_gather(w_keyval.astype(jnp.bfloat16), ('clus', 'fsdp'), axis=0, t...]
    ppermute x0 -> x26, starting transfers between devices: none -> 49.8 us  [the longest x20 45.5 us: shift(): return lax.ppermute(x, 'fsdp', pairs)]
    dot_general x12 -> x0, matrix products: 37.6 us -> none  [the longest x1 5.7 us: on_device(): grad_table = jnp.dot(onehot.T, dkeys, precision=lax.Precision.HIGHEST)]
    pallas_call x0 -> x6, Pallas kernels: none -> 37.3 us  [the longest x2 29 us: in_plane(): pl.pallas_call(head_kernel, in_specs=[SMEM] * 3 + [ANY] * 13, out_specs=[...]
    all_to_all x0 -> x1, blocking collectives: none -> 20.7 us  [in_plane(): own_w = [lax.all_to_all(x, 'clus', 0, 0, tiled=True) for x in parts]]
    all_to_all x2 -> x7, starting transfers between devices: 7.3 us -> 27.4 us  [the longest x2 7.88 us: in_plane(): lax.all_to_all(out.reshape(nclus, rows, HD), 'clus', 0, 0, tiled=True)]
    unnamed x37 -> x53, local copies, waits for them, and re-layouts: 17.6 us -> 5.58 us
  transfers between devices with their start and end apart: 6 -> 33, of which waited for: 5 -> 9; matrix products, arithmetic and copies ran while one was open for 8% -> 4% of each run, Pallas kernels for 0% -> 19%
where the time goes in v1:
time: 175 us; the launch traced here: 172 us
  starting transfers between devices  77.2 us (44%)
  Pallas kernels  37.3 us (21%)
  waiting for transfers between devices  24.1 us (14%)
  blocking collectives  20.7 us (12%)
  local copies, waits for them, and re-layouts  6.4 us (4%)
  other arithmetic  5.34 us (3%)
    ppermute x20, starting transfers between devices, shift(): return lax.ppermute(x, 'fsdp', pairs)  45.5 us
    pallas_call x2, Pallas kernels, in_plane(): pl.pallas_call(head_kernel, in_specs=[SMEM] * 3 + [ANY] * 13, out_specs=[...  29 us
    all_to_all x1, blocking collectives, in_plane(): own_w = [lax.all_to_all(x, 'clus', 0, 0, tiled=True) for x in parts]  20.7 us
    ppermute x20, waiting for transfers between devices, shift(): return lax.ppermute(x, 'fsdp', pairs)  8.66 us
    all_to_all x2, starting transfers between devices, in_plane(): lax.all_to_all(out.reshape(nclus, rows, HD), 'clus', 0, 0, tiled=True)  7.88 us
    all_to_all x2, waiting for transfers between devices, in_plane(): grads.append(lax.all_to_all(total, 'clus', 0, 0, tiled=True))  7.87 us
    all_to_all x2, starting transfers between devices, in_plane(): grads.append(lax.all_to_all(total, 'clus', 0, 0, tiled=True))  7.41 us
    all_to_all x2, starting transfers between devices, in_plane(): lax.all_to_all(x, 'clus', 0, 0, tiled=True).reshape(nodes, HD)  6.95 us
  transfers between devices with their start and end apart: 33, of which 9 were waited for; matrix products, arithmetic and copies ran while one was open for 4% of the time, Pallas kernels for 19%

profile of v1, /device:TPU:0, one launch (start us, length us, event | category | flops | bytes accessed | tf_op | source)
XLA Modules:
  0.0 172.2 jit_solution(1047816864873403228)
XLA Ops:
  0.6 2.1 %split_weights.1 = (bf16[4,128,256]{2,1,0:T(8,128)(2,1)}, bf16[4,128,256]{2,1,0:T(8,128)(2,1)}) custom-call(f32[128,1024]{1,0:T(8,128)} %wq_ref.1, f32[128,1024]{1,0:T(8,128)} %wkv_ref.1), custom_call_target="tpu_custom_call" | custom-call | tf_op jit(solution)/shard_map/split_weights/pallas_call | solution.py:208
  2.8 5.2 %all-to-all-start.3 = ((bf16[4,128,256]{2,1,0:T(8,128)(2,1)}), bf16[4,128,256]{2,1,0:T(8,128)(2,1)S(1)}, u32[]{:S(2)}, u32[]{:S(2)}) async-start(bf16[4,128,256]{2,1,0:T(8,128)(2,1)} %get-tuple-element.22), calls=%async_computation.3 | async-start | bytes 524288 | tf_op jit(solution)/shard_map/all_to_all | solution.py:215
  11.6 2.9 %all-to-all-done.3.w0_ref = bf16[4,128,256]{2,1,0:T(8,128)(2,1)S(1)} async-done(((bf16[4,128,256]{2,1,0:T(8,128)(2,1)}), bf16[4,128,256]{2,1,0:T(8,128)(2,1)S(1)}, u32[]{:S(2)}, u32[]{:S(2)}) %all-to-all-start.3) | async-done | bytes 262176 | tf_op jit(solution)/shard_map/all_to_all | solution.py:215
  16.1 2.2 %collective-permute-start.11 = (bf16[4,128,256]{2,1,0:T(8,128)(2,1)S(1)}, bf16[4,128,256]{2,1,0:T(8,128)(2,1)S(1)}, u32[]{:S(2)}, u32[]{:S(2)}) collective-permute-start(bf16[4,128,256]{2,1,0:T(8,128)(2,1)S(1)} %all-to-all-done.3.w0_ref), channel_id=1, source_target_pairs={{0,6},{2,0},{4,2},{6,4},{1,7},{3,1},{5,3},{7,5},{8,14},{10,8},{12,... | collective-permute-start | bytes 786440 | tf_op jit(solution)/shard_map/ppermute | solution.py:204
  18.4 20.7 %all_to_all.40.w0_ref = bf16[4,128,256]{2,1,0:T(8,128)(2,1)} all-to-all(bf16[4,128,256]{2,1,0:T(8,128)(2,1)S(1)} %copy-done.20), channel_id=1, replica_groups=mesh['clus'=4,'fsdp'=4,'head'=2] {'clus'}, dimensions={0} | all-to-all | bytes 524288 | tf_op jit(solution)/shard_map/all_to_all | solution.py:215
  40.7 2.2 %collective-permute-start.7 = (bf16[4,128,256]{2,1,0:T(8,128)(2,1)}, bf16[4,128,256]{2,1,0:T(8,128)(2,1)}, u32[]{:S(2)}, u32[]{:S(2)}) collective-permute-start(bf16[4,128,256]{2,1,0:T(8,128)(2,1)} %all_to_all.40.w0_ref), channel_id=1, source_target_pairs={{0,6},{2,0},{4,2},{6,4},{1,7},{3,1},{5,3},{7,5},{8,14},{10,8},{12,... | collective-permute-start | bytes 786440 | tf_op jit(solution)/shard_map/ppermute | solution.py:204
  45.8 3.4 %all-to-all-start.4 = ((bf16[4,256,128]{2,1,0:T(8,128)(2,1)}), bf16[4,256,128]{2,1,0:T(8,128)(2,1)S(1)}, u32[]{:S(2)}, u32[]{:S(2)}) async-start(bf16[4,256,128]{2,1,0:T(8,128)(2,1)} %get-tuple-element.23), calls=%async_computation.4 | async-start | bytes 524288 | tf_op jit(solution)/shard_map/all_to_all | solution.py:226
  56.9 7.0 %collective-permute-done.13.wfar_dn_ref = bf16[4,128,256]{2,1,0:T(8,128)(2,1)} collective-permute-done((bf16[4,128,256]{2,1,0:T(8,128)(2,1)}, bf16[4,128,256]{2,1,0:T(8,128)(2,1)}, u32[]{:S(2)}, u32[]{:S(2)}) %collective-permute-start.13) | collective-permute-done | bytes 262176 | tf_op jit(solution)/shard_map/ppermute | solution.py:204
  67.1 14.4 %heads.3 = (bf16[1024,128]{1,0:T(8,128)(2,1)}, bf16[4,256,128]{2,1,0:T(8,128)(2,1)}, bf16[4,256,128]{2,1,0:T(8,128)(2,1)}, bf16[4,256,128]{2,1,0:T(8,128)(2,1)}, bf16[4,256,128]{2,1,0:T(8,128)(2,1)}) custom-call(s32[3]{0:T(128)} %pad_add_fusion.pos_ref, s32[8,5]{1,0:T(8,128)} %fusion.2.cols_ref, s32[8]{0:T(128)} %reshape.35.counts_ref, ...), custom_call_target="tpu_custom_call" | custom-call | tf_op jit(solution)/shard_map/heads/pallas_call | solution.py:243
  81.5 4.6 %collective-permute-start.20 = (bf16[4,256,128]{2,1,0:T(8,128)(2,1)}, bf16[4,256,128]{2,1,0:T(8,128)(2,1)S(1)}, u32[]{:S(2)}, u32[]{:S(2)}) collective-permute-start(bf16[4,256,128]{2,1,0:T(8,128)(2,1)} %get-tuple-element.31), channel_id=1, source_target_pairs={{0,2},{2,4},{1,3},{3,5},{8,10},{10,12},{9,11},{11,13},{16,18},{18,... | collective-permute-start | bytes 786440 | tf_op jit(solution)/shard_map/ppermute | solution.py:204
  86.2 3.5 %all-to-all-start.1 = ((bf16[4,256,128]{2,1,0:T(8,128)(2,1)}), bf16[4,256,128]{2,1,0:T(8,128)(2,1)S(1)}, u32[]{:S(2)}, u32[]{:S(2)}) async-start(bf16[4,256,128]{2,1,0:T(8,128)(2,1)} %get-tuple-element.20), calls=%async_computation.1 | async-start | bytes 524288 | tf_op jit(solution)/shard_map/all_to_all | solution.py:226
  90.6 4.5 %all-to-all-done.1 = bf16[4,256,128]{2,1,0:T(8,128)(2,1)S(1)} async-done(((bf16[4,256,128]{2,1,0:T(8,128)(2,1)}), bf16[4,256,128]{2,1,0:T(8,128)(2,1)S(1)}, u32[]{:S(2)}, u32[]{:S(2)}) %all-to-all-start.1) | async-done | bytes 262176 | tf_op jit(solution)/shard_map/all_to_all | solution.py:226
  95.8 14.6 %heads.2 = (bf16[1024,128]{1,0:T(8,128)(2,1)}, bf16[4,256,128]{2,1,0:T(8,128)(2,1)}, bf16[4,256,128]{2,1,0:T(8,128)(2,1)}, bf16[4,256,128]{2,1,0:T(8,128)(2,1)}, bf16[4,256,128]{2,1,0:T(8,128)(2,1)}) custom-call(s32[3]{0:T(128)} %pad_add_fusion.pos_ref, s32[8,5]{1,0:T(8,128)} %fusion.2.cols_ref, s32[8]{0:T(128)} %reshape.35.counts_ref, ...), custom_call_target="tpu_custom_call" | custom-call | tf_op jit(solution)/shard_map/heads/pallas_call | solution.py:243
  110.4 4.6 %collective-permute-start.14 = (bf16[4,256,128]{2,1,0:T(8,128)(2,1)}, bf16[4,256,128]{2,1,0:T(8,128)(2,1)S(1)}, u32[]{:S(2)}, u32[]{:S(2)}) collective-permute-start(bf16[4,256,128]{2,1,0:T(8,128)(2,1)} %get-tuple-element.27), channel_id=1, source_target_pairs={{0,2},{2,4},{1,3},{3,5},{8,10},{10,12},{9,11},{11,13},{16,18},{18,... | collective-permute-start | bytes 786440 | tf_op jit(solution)/shard_map/ppermute | solution.py:204
  115.7 2.8 %collective-permute-start.24 = (bf16[4,256,128]{2,1,0:T(8,128)(2,1)S(1)}, bf16[4,256,128]{2,1,0:T(8,128)(2,1)S(1)}, u32[]{:S(2)}, u32[]{:S(2)}) collective-permute-start(bf16[4,256,128]{2,1,0:T(8,128)(2,1)S(1)} %copy-done.19), channel_id=1, source_target_pairs={{0,6},{1,7},{8,14},{9,15},{16,22},{17,23},{24,30},{25,31}} | collective-permute-start | bytes 786440 | tf_op jit(solution)/shard_map/ppermute | solution.py:204
  118.5 3.7 %all-to-all-start.5 = ((bf16[4,256,128]{2,1,0:T(8,128)(2,1)}), bf16[4,256,128]{2,1,0:T(8,128)(2,1)S(1)}, u32[]{:S(2)}, u32[]{:S(2)}) async-start(bf16[4,256,128]{2,1,0:T(8,128)(2,1)} %bitcast.8), calls=%async_computation.5 | async-start | bytes 524288 | tf_op jit(solution)/shard_map/all_to_all | solution.py:261
  123.6 2.2 %collective-permute-start.21 = (bf16[4,256,128]{2,1,0:T(8,128)(2,1)S(1)}, bf16[4,256,128]{2,1,0:T(8,128)(2,1)}, u32[]{:S(2)}, u32[]{:S(2)}) collective-permute-start(bf16[4,256,128]{2,1,0:T(8,128)(2,1)S(1)} %add_convert_fusion.2), channel_id=1, source_target_pairs={{0,2},{2,4},{4,6},{1,3},{3,5},{5,7},{8,10},{10,12},{12,14},{9,11},... | collective-permute-start | bytes 786440 | tf_op jit(solution)/shard_map/ppermute | solution.py:204
  127.3 9.6 %collective-permute-start.18 = (bf16[4,256,128]{2,1,0:T(8,128)(2,1)S(1)}, bf16[4,256,128]{2,1,0:T(8,128)(2,1)S(1)}, u32[]{:S(2)}, u32[]{:S(2)}) collective-permute-start(bf16[4,256,128]{2,1,0:T(8,128)(2,1)S(1)} %copy-done.17), channel_id=1, source_target_pairs={{0,6},{1,7},{8,14},{9,15},{16,22},{17,23},{24,30},{25,31}} | collective-permute-start | bytes 786440 | tf_op jit(solution)/shard_map/ppermute | solution.py:204
  139.0 4.2 %all-to-all-start.2 = ((bf16[4,256,128]{2,1,0:T(8,128)(2,1)}), bf16[4,256,128]{2,1,0:T(8,128)(2,1)S(1)}, u32[]{:S(2)}, u32[]{:S(2)}) async-start(bf16[4,256,128]{2,1,0:T(8,128)(2,1)} %bitcast.6), calls=%async_computation.2 | async-start | bytes 524288 | tf_op jit(solution)/shard_map/all_to_all | solution.py:261
  149.3 4.0 %all-to-all-start.7 = ((bf16[4,256,128]{2,1,0:T(8,128)(2,1)}), bf16[4,256,128]{2,1,0:T(8,128)(2,1)S(1)}, u32[]{:S(2)}, u32[]{:S(2)}) async-start(bf16[4,256,128]{2,1,0:T(8,128)(2,1)} %add_convert_fusion), calls=%async_computation.7 | async-start | bytes 524288 | tf_op jit(solution)/shard_map/all_to_all | solution.py:269
  155.3 4.5 %all-to-all-done.7.refs_1_ = bf16[4,256,128]{2,1,0:T(8,128)(2,1)S(1)} async-done(((bf16[4,256,128]{2,1,0:T(8,128)(2,1)}), bf16[4,256,128]{2,1,0:T(8,128)(2,1)S(1)}, u32[]{:S(2)}, u32[]{:S(2)}) %all-to-all-start.7) | async-done | bytes 262176 | tf_op jit(solution)/shard_map/all_to_all | solution.py:269
  160.5 3.4 %all-to-all-start.6 = ((bf16[4,256,128]{2,1,0:T(8,128)(2,1)}), bf16[4,256,128]{2,1,0:T(8,128)(2,1)S(1)}, u32[]{:S(2)}, u32[]{:S(2)}) async-start(bf16[4,256,128]{2,1,0:T(8,128)(2,1)} %add_convert_fusion.3), calls=%async_computation.6 | async-start | bytes 524288 | tf_op jit(solution)/shard_map/all_to_all | solution.py:269
  165.9 3.4 %all-to-all-done.6.refs_0_ = bf16[4,256,128]{2,1,0:T(8,128)(2,1)S(1)} async-done(((bf16[4,256,128]{2,1,0:T(8,128)(2,1)}), bf16[4,256,128]{2,1,0:T(8,128)(2,1)S(1)}, u32[]{:S(2)}, u32[]{:S(2)}) %all-to-all-start.6) | async-done | bytes 262176 | tf_op jit(solution)/shard_map/all_to_all | solution.py:269
  170.0 2.2 %merge_grads.1 = (f32[128,1024]{1,0:T(8,128)}, f32[128,1024]{1,0:T(8,128)}) custom-call(bf16[4,256,128]{2,1,0:T(8,128)(2,1)} %copy-done.11, bf16[4,256,128]{2,1,0:T(8,128)(2,1)} %copy-done.10), custom_call_target="tpu_custom_call" | custom-call | tf_op jit(solution)/shard_map/merge_grads/pallas_call | solution.py:277
  (115 shorter events, 39.1 us)
Async XLA Ops:
  2.8 11.8 %all-to-all-start.3 = ((bf16[4,128,256]{2,1,0:T(8,128)(2,1)}), bf16[4,128,256]{2,1,0:T(8,128)(2,1)S(1)}, u32[]{:S(2)}, u32[]{:S(2)}) async-start(bf16[4,128,256]{2,1,0:T(8,128)(2,1)} %get-tuple-element.22), calls=%async_computation.3 | async-start | bytes 524288 | tf_op jit(solution)/shard_map/all_to_all | solution.py:215
  8.0 35.0 %collective-permute-start = (bf16[256,1024]{1,0:T(8,128)(2,1)S(1)}, bf16[256,1024]{1,0:T(8,128)(2,1)S(1)}, u32[]{:S(2)}, u32[]{:S(2)}) collective-permute-start(bf16[256,1024]{1,0:T(8,128)(2,1)S(1)} %constant_dynamic-slice_fusion), channel_id=1, source_target_pairs={{0,8},{8,0},{16,24},{24,16},{1,9},{9,1},{17,25},{25,17},{2,10},{10... | collective-permute-start | bytes 1572872 | tf_op jit(solution)/shard_map/ppermute | solution.py:217
  10.1 33.0 %collective-permute-start.1 = (bf16[256,1024]{1,0:T(8,128)(2,1)S(1)}, bf16[256,1024]{1,0:T(8,128)(2,1)S(1)}, u32[]{:S(2)}, u32[]{:S(2)}) collective-permute-start(bf16[256,1024]{1,0:T(8,128)(2,1)S(1)} %constant_dynamic-slice_fusion), channel_id=1, source_target_pairs={{0,16},{8,24},{16,0},{24,8},{1,17},{9,25},{17,1},{25,9},{2,18},{10... | collective-permute-start | bytes 1572872 | tf_op jit(solution)/shard_map/ppermute | solution.py:217
  11.6 32.1 %collective-permute-start.2 = (bf16[256,1024]{1,0:T(8,128)(2,1)S(1)}, bf16[256,1024]{1,0:T(8,128)(2,1)S(1)}, u32[]{:S(2)}, u32[]{:S(2)}) collective-permute-start(bf16[256,1024]{1,0:T(8,128)(2,1)S(1)} %constant_dynamic-slice_fusion), channel_id=1, source_target_pairs={{0,24},{8,16},{16,8},{24,0},{1,25},{9,17},{17,9},{25,1},{2,26},{10... | collective-permute-start | bytes 1572872 | tf_op jit(solution)/shard_map/ppermute | solution.py:217
  14.5 24.6 %collective-permute-start.10 = (bf16[4,128,256]{2,1,0:T(8,128)(2,1)S(1)}, bf16[4,128,256]{2,1,0:T(8,128)(2,1)S(1)}, u32[]{:S(2)}, u32[]{:S(2)}) collective-permute-start(bf16[4,128,256]{2,1,0:T(8,128)(2,1)S(1)} %all-to-all-done.3.w0_ref), channel_id=1, source_target_pairs={{0,2},{2,4},{4,6},{6,0},{1,3},{3,5},{5,7},{7,1},{8,10},{10,12},{12... | collective-permute-start | bytes 786440 | tf_op jit(solution)/shard_map/ppermute | solution.py:204
  16.1 24.6 %collective-permute-start.11 = (bf16[4,128,256]{2,1,0:T(8,128)(2,1)S(1)}, bf16[4,128,256]{2,1,0:T(8,128)(2,1)S(1)}, u32[]{:S(2)}, u32[]{:S(2)}) collective-permute-start(bf16[4,128,256]{2,1,0:T(8,128)(2,1)S(1)} %all-to-all-done.3.w0_ref), channel_id=1, source_target_pairs={{0,6},{2,0},{4,2},{6,4},{1,7},{3,1},{5,3},{7,5},{8,14},{10,8},{12,... | collective-permute-start | bytes 786440 | tf_op jit(solution)/shard_map/ppermute | solution.py:204
  39.1 11.4 %collective-permute-start.6 = (bf16[4,128,256]{2,1,0:T(8,128)(2,1)}, bf16[4,128,256]{2,1,0:T(8,128)(2,1)}, u32[]{:S(2)}, u32[]{:S(2)}) collective-permute-start(bf16[4,128,256]{2,1,0:T(8,128)(2,1)} %all_to_all.40.w0_ref), channel_id=1, source_target_pairs={{0,2},{2,4},{4,6},{6,0},{1,3},{3,5},{5,7},{7,1},{8,10},{10,12},{12... | collective-permute-start | bytes 786440 | tf_op jit(solution)/shard_map/ppermute | solution.py:204
  40.7 12.1 %collective-permute-start.7 = (bf16[4,128,256]{2,1,0:T(8,128)(2,1)}, bf16[4,128,256]{2,1,0:T(8,128)(2,1)}, u32[]{:S(2)}, u32[]{:S(2)}) collective-permute-start(bf16[4,128,256]{2,1,0:T(8,128)(2,1)} %all_to_all.40.w0_ref), channel_id=1, source_target_pairs={{0,6},{2,0},{4,2},{6,4},{1,7},{3,1},{5,3},{7,5},{8,14},{10,8},{12,... | collective-permute-start | bytes 786440 | tf_op jit(solution)/shard_map/ppermute | solution.py:204
  43.0 22.9 %collective-permute-start.3 = (bf16[256,1024]{1,0:T(8,128)(2,1)S(1)}, bf16[256,1024]{1,0:T(8,128)(2,1)S(1)}, u32[]{:S(2)}, u32[]{:S(2)}) collective-permute-start(bf16[256,1024]{1,0:T(8,128)(2,1)S(1)} %collective-permute-done.mine1_ref), channel_id=1, source_target_pairs={{0,1},{1,0},{2,3},{3,2},{4,5},{5,4},{6,7},{7,6},{8,9},{9,8},{10,11... | collective-permute-start | bytes 1572872 | tf_op jit(solution)/shard_map/ppermute | solution.py:218
  43.1 22.8 %collective-permute-start.4 = (bf16[256,1024]{1,0:T(8,128)(2,1)S(1)}, bf16[256,1024]{1,0:T(8,128)(2,1)S(1)}, u32[]{:S(2)}, u32[]{:S(2)}) collective-permute-start(bf16[256,1024]{1,0:T(8,128)(2,1)S(1)} %collective-permute-done.1.mine2_ref), channel_id=1, source_target_pairs={{0,1},{1,0},{2,3},{3,2},{4,5},{5,4},{6,7},{7,6},{8,9},{9,8},{10,11... | collective-permute-start | bytes 1572872 | tf_op jit(solution)/shard_map/ppermute | solution.py:218
  43.6 22.2 %collective-permute-start.5 = (bf16[256,1024]{1,0:T(8,128)(2,1)S(1)}, bf16[256,1024]{1,0:T(8,128)(2,1)S(1)}, u32[]{:S(2)}, u32[]{:S(2)}) collective-permute-start(bf16[256,1024]{1,0:T(8,128)(2,1)S(1)} %collective-permute-done.2.mine3_ref), channel_id=1, source_target_pairs={{0,1},{1,0},{2,3},{3,2},{4,5},{5,4},{6,7},{7,6},{8,9},{9,8},{10,11... | collective-permute-start | bytes 1572872 | tf_op jit(solution)/shard_map/ppermute | solution.py:218
  45.8 20.1 %all-to-all-start.4 = ((bf16[4,256,128]{2,1,0:T(8,128)(2,1)}), bf16[4,256,128]{2,1,0:T(8,128)(2,1)S(1)}, u32[]{:S(2)}, u32[]{:S(2)}) async-start(bf16[4,256,128]{2,1,0:T(8,128)(2,1)} %get-tuple-element.23), calls=%async_computation.4 | async-start | bytes 524288 | tf_op jit(solution)/shard_map/all_to_all | solution.py:226
  55.5 39.6 %collective-permute-start.8 = (bf16[4,128,256]{2,1,0:T(8,128)(2,1)}, bf16[4,128,256]{2,1,0:T(8,128)(2,1)}, u32[]{:S(2)}, u32[]{:S(2)}) collective-permute-start(bf16[4,128,256]{2,1,0:T(8,128)(2,1)} %collective-permute-done.6.wup_ref), channel_id=1, source_target_pairs={{2,4},{4,6},{3,5},{5,7},{10,12},{12,14},{11,13},{13,15},{18,20},{2... | collective-permute-start | bytes 786440 | tf_op jit(solution)/shard_map/ppermute | solution.py:204
  63.9 31.2 %collective-permute-start.9 = (bf16[4,128,256]{2,1,0:T(8,128)(2,1)}, bf16[4,128,256]{2,1,0:T(8,128)(2,1)}, u32[]{:S(2)}, u32[]{:S(2)}) collective-permute-start(bf16[4,128,256]{2,1,0:T(8,128)(2,1)} %collective-permute-done.7.wdn_ref), channel_id=1, source_target_pairs={{4,2},{2,0},{5,3},{3,1},{12,10},{10,8},{13,11},{11,9},{20,18},{18,... | collective-permute-start | bytes 786440 | tf_op jit(solution)/shard_map/ppermute | solution.py:204
  81.5 40.7 %collective-permute-start.20 = (bf16[4,256,128]{2,1,0:T(8,128)(2,1)}, bf16[4,256,128]{2,1,0:T(8,128)(2,1)S(1)}, u32[]{:S(2)}, u32[]{:S(2)}) collective-permute-start(bf16[4,256,128]{2,1,0:T(8,128)(2,1)} %get-tuple-element.31), channel_id=1, source_target_pairs={{0,2},{2,4},{1,3},{3,5},{8,10},{10,12},{9,11},{11,13},{16,18},{18,... | collective-permute-start | bytes 786440 | tf_op jit(solution)/shard_map/ppermute | solution.py:204
  89.7 33.9 %collective-permute-start.22 = (bf16[4,256,128]{2,1,0:T(8,128)(2,1)S(1)}, bf16[4,256,128]{2,1,0:T(8,128)(2,1)S(1)}, u32[]{:S(2)}, u32[]{:S(2)}) collective-permute-start(bf16[4,256,128]{2,1,0:T(8,128)(2,1)S(1)} %copy-done.25), channel_id=1, source_target_pairs={{6,4},{4,2},{7,5},{5,3},{14,12},{12,10},{15,13},{13,11},{22,20},{2... | collective-permute-start | bytes 786440 | tf_op jit(solution)/shard_map/ppermute | solution.py:204
  110.4 16.9 %collective-permute-start.14 = (bf16[4,256,128]{2,1,0:T(8,128)(2,1)}, bf16[4,256,128]{2,1,0:T(8,128)(2,1)S(1)}, u32[]{:S(2)}, u32[]{:S(2)}) collective-permute-start(bf16[4,256,128]{2,1,0:T(8,128)(2,1)} %get-tuple-element.27), channel_id=1, source_target_pairs={{0,2},{2,4},{1,3},{3,5},{8,10},{10,12},{9,11},{11,13},{16,18},{18,... | collective-permute-start | bytes 786440 | tf_op jit(solution)/shard_map/ppermute | solution.py:204
  115.7 21.3 %collective-permute-start.24 = (bf16[4,256,128]{2,1,0:T(8,128)(2,1)S(1)}, bf16[4,256,128]{2,1,0:T(8,128)(2,1)S(1)}, u32[]{:S(2)}, u32[]{:S(2)}) collective-permute-start(bf16[4,256,128]{2,1,0:T(8,128)(2,1)S(1)} %copy-done.19), channel_id=1, source_target_pairs={{0,6},{1,7},{8,14},{9,15},{16,22},{17,23},{24,30},{25,31}} | collective-permute-start | bytes 786440 | tf_op jit(solution)/shard_map/ppermute | solution.py:204
  118.5 19.8 %all-to-all-start.5 = ((bf16[4,256,128]{2,1,0:T(8,128)(2,1)}), bf16[4,256,128]{2,1,0:T(8,128)(2,1)S(1)}, u32[]{:S(2)}, u32[]{:S(2)}) async-start(bf16[4,256,128]{2,1,0:T(8,128)(2,1)} %bitcast.8), calls=%async_computation.5 | async-start | bytes 524288 | tf_op jit(solution)/shard_map/all_to_all | solution.py:261
  122.2 20.9 %collective-permute-start.25 = (bf16[4,256,128]{2,1,0:T(8,128)(2,1)S(1)}, bf16[4,256,128]{2,1,0:T(8,128)(2,1)S(1)}, u32[]{:S(2)}, u32[]{:S(2)}) collective-permute-start(bf16[4,256,128]{2,1,0:T(8,128)(2,1)S(1)} %copy-done.18), channel_id=1, source_target_pairs={{6,0},{7,1},{14,8},{15,9},{22,16},{23,17},{30,24},{31,25}} | collective-permute-start | bytes 786440 | tf_op jit(solution)/shard_map/ppermute | solution.py:204
  123.6 21.5 %collective-permute-start.21 = (bf16[4,256,128]{2,1,0:T(8,128)(2,1)S(1)}, bf16[4,256,128]{2,1,0:T(8,128)(2,1)}, u32[]{:S(2)}, u32[]{:S(2)}) collective-permute-start(bf16[4,256,128]{2,1,0:T(8,128)(2,1)S(1)} %add_convert_fusion.2), channel_id=1, source_target_pairs={{0,2},{2,4},{4,6},{1,3},{3,5},{5,7},{8,10},{10,12},{12,14},{9,11},... | collective-permute-start | bytes 786440 | tf_op jit(solution)/shard_map/ppermute | solution.py:204
  125.9 20.6 %collective-permute-start.23 = (bf16[4,256,128]{2,1,0:T(8,128)(2,1)S(1)}, bf16[4,256,128]{2,1,0:T(8,128)(2,1)}, u32[]{:S(2)}, u32[]{:S(2)}) collective-permute-start(bf16[4,256,128]{2,1,0:T(8,128)(2,1)S(1)} %add_convert_fusion.1), channel_id=1, source_target_pairs={{6,4},{4,2},{2,0},{7,5},{5,3},{3,1},{14,12},{12,10},{10,8},{15,13}... | collective-permute-start | bytes 786440 | tf_op jit(solution)/shard_map/ppermute | solution.py:204
  127.3 26.0 %collective-permute-start.18 = (bf16[4,256,128]{2,1,0:T(8,128)(2,1)S(1)}, bf16[4,256,128]{2,1,0:T(8,128)(2,1)S(1)}, u32[]{:S(2)}, u32[]{:S(2)}) collective-permute-start(bf16[4,256,128]{2,1,0:T(8,128)(2,1)S(1)} %copy-done.17), channel_id=1, source_target_pairs={{0,6},{1,7},{8,14},{9,15},{16,22},{17,23},{24,30},{25,31}} | collective-permute-start | bytes 786440 | tf_op jit(solution)/shard_map/ppermute | solution.py:204
  137.0 16.3 %collective-permute-start.19 = (bf16[4,256,128]{2,1,0:T(8,128)(2,1)S(1)}, bf16[4,256,128]{2,1,0:T(8,128)(2,1)}, u32[]{:S(2)}, u32[]{:S(2)}) collective-permute-start(bf16[4,256,128]{2,1,0:T(8,128)(2,1)S(1)} %copy-done.16), channel_id=1, source_target_pairs={{6,0},{7,1},{14,8},{15,9},{22,16},{23,17},{30,24},{31,25}} | collective-permute-start | bytes 786440 | tf_op jit(solution)/shard_map/ppermute | solution.py:204
  (35 other events, 221.8 us)
